TPU v7x, 32 devices: a whole 2x2x4 slice. The times are simulated.
32 devices in a mesh: dp: 4 (over z), expert: 8 (over y, x, core).
Axes of the slice: x: 2, y: 2, z: 4, core: 2. Of those that a mesh axis runs over, the one named last changes fastest.
Arguments:
- out_grad: bfloat16 [8192, 4096], P(('dp', 'expert')), may hold values from -6 to 6
- destination: int32 [8192, 1], P(('dp', 'expert')), may hold values from 0 to 7; in each aligned block of 256 rows (0 to 255, 256 to 511, ...) at most 64 rows name the same one
- hidden: bfloat16 [16384, 1024], P(('dp', 'expert')), may hold values from -6 to 6
- weight: bfloat16 [8, 1024, 4096], P('expert', None, 'dp'), may hold values from -0.09375 to 0.09375
- left_prev: float32 [8, 2048, 1024], P('expert', 'dp'), may hold values from -3 to 3
- right_prev: float32 [8, 4096, 2048], P('expert', 'dp'), may hold values from -3 to 3
Outputs:
- grad_rows: bfloat16 [8192, 1024], P(('dp', 'expert'))
- left_stats: float32 [8, 2048, 1024], P('expert', 'dp')
- right_stats: float32 [8, 4096, 2048], P('expert', 'dp')
Inputs may be any that keep to these rules, and one draw needn't show every extreme that they name: Among the rows of one device at most 64 have the same destination, and on some device that many do.
All inputs are finite; a program needn't handle non-finite values.
Results may differ from a plain program's by a relative error of at most 0.001.
Values may be sent and summed in bfloat16 or wider, within the bound.
A program may use at most 128 MiB of HBM per device.

v0:
```python
import jax
import jax.numpy as jnp
from jax import lax
from jax.sharding import PartitionSpec as P

ema_decay = 0.9


def swapped(value, axis, distance):
    mask = 2**distance
    pairs = [(source, source ^ mask) for source in range(lax.axis_size(axis))]
    return lax.ppermute(value, axis, pairs)


def slot_places(dest_column, expert_count, capacity):
    choose = (dest_column[:, None] == jnp.arange(expert_count, dtype=jnp.int32)[None, :]).astype(
        jnp.int32
    )
    before = jnp.cumsum(choose, axis=0) - choose
    slot_rank = jnp.sum(before * choose, axis=1)
    return dest_column * capacity + slot_rank


def local(out_grad, destination, hidden, weight, left_prev, right_prev):
    expert_count = lax.axis_size("expert")
    group_count = lax.axis_size("dp")
    row_count, model_width = out_grad.shape
    slot_count, hidden_width = hidden.shape
    capacity = slot_count // expert_count
    target_slots = slot_places(destination[:, 0], expert_count, capacity)
    outgoing = jnp.zeros((slot_count, model_width), out_grad.dtype).at[target_slots].set(out_grad)
    arrived = lax.all_to_all(
        outgoing.reshape(expert_count, capacity, model_width),
        "expert",
        split_axis=0,
        concat_axis=0,
        tiled=True,
    )
    arrived = arrived.reshape(slot_count, model_width)
    columns = arrived
    slot_grad = lax.dot_general(
        columns,
        lax.all_gather(weight[0], "dp", axis=1, tiled=True),
        (((1,), (1,)), ((), ())),
        preferred_element_type=jnp.float32,
    ).astype(jnp.bfloat16)
    returned = lax.all_to_all(
        slot_grad.reshape(expert_count, capacity, hidden_width),
        "expert",
        split_axis=0,
        concat_axis=0,
        tiled=True,
    )
    grad_rows = returned.reshape(slot_count, hidden_width)[target_slots]
    half_width = model_width // group_count
    block_width = 2 * half_width
    columns_all = lax.all_to_all(arrived, "dp", split_axis=1, concat_axis=0, tiled=True)
    columns = columns_all
    own_piece = lax.dot_general(
        columns,
        lax.all_gather(hidden, "dp", axis=0, tiled=True),
        (((0,), (0,)), ((), ())),
        preferred_element_type=jnp.float32,
    )
    partner = swapped(own_piece.astype(jnp.bfloat16), "dp", 0).astype(own_piece.dtype)
    parity = lax.axis_index("dp") % 2
    upper_half = parity == 0
    first_half = jnp.where(upper_half, own_piece, partner)
    second_half = jnp.where(upper_half, partner, own_piece)
    block_grad = jnp.concatenate([first_half, second_half], axis=0)
    scale_left = 1.0 / (group_count * row_count * block_width)
    scale_right = 1.0 / (group_count * row_count * hidden_width)
    right_gram = (
        lax.dot_general(
            own_piece,
            block_grad,
            (((1,), (1,)), ((), ())),
            precision=lax.Precision.HIGHEST,
            preferred_element_type=jnp.float32,
        )
        * scale_right
    )
    half_hidden = hidden_width // 2
    hidden_cols = lax.dynamic_slice_in_dim(block_grad, parity * half_hidden, half_hidden, 1)
    left_gram = (
        lax.dot_general(
            hidden_cols,
            block_grad,
            (((0,), (0,)), ((), ())),
            precision=lax.Precision.HIGHEST,
            preferred_element_type=jnp.float32,
        )
        * scale_left
    )
    left_stats = ema_decay * left_prev + (1.0 - ema_decay) * left_gram[None]
    right_stats = ema_decay * right_prev + (1.0 - ema_decay) * right_gram[None]
    return (grad_rows, left_stats, right_stats)


def solution(mesh):
    placed = (
        P(("dp", "expert"), None),
        P(("dp", "expert"), None),
        P(("dp", "expert"), None),
        P("expert", None, "dp"),
        P("expert", "dp", None),
        P("expert", "dp", None),
    )
    return jax.shard_map(
        local,
        mesh=mesh,
        in_specs=placed,
        out_specs=(P(("dp", "expert"), None), P("expert", "dp", None), P("expert", "dp", None)),
        check_vma=False,
    )
```

profile of v0, /device:TPU:1, one launch (start us, length us, event | category | flops | bytes accessed | tf_op | source)
XLA Modules:
  0.0 439.9 jit_solution(14873368726343647602)
XLA Ops:
  7.2 0.0 all-gather.4.cloned.1.call-start
  7.2 0.7 all-gather.4.cloned.1.call-update
  7.9 0.7 fusion.15
  8.6 0.6 reduce-window.6
  9.2 0.2 slice_reduce_fusion
  9.4 0.8 fusion.14
  10.2 0.7 compare_select_fusion
  10.9 7.1 %scatter_custom_fusion = bf16[512,4096]{1,0:T(8,128)(2,1)} fusion(s32[256]{0:T(256)S(1)} %bitcast.37, bf16[256,4096]{1,0:T(8,128)(2,1)} %param.6, bf16[]{:T(256)} %constant.14.clone.1), kind=kCustom, calls=%fused_computation.14 | custom fusion | bytes 4194816 | tf_op jit(solution)/shard_map/scatter | solution.py:31
  18.0 5.2 %all-to-all-start = ((bf16[8,64,4096]{2,1,0:T(8,128)(2,1)}), bf16[8,64,4096]{2,1,0:T(8,128)(2,1)}, u32[]{:S(2)}, u32[]{:S(2)}) async-start(bf16[8,64,4096]{2,1,0:T(8,128)(2,1)} %bitcast.34), calls=%async_computation | async-start | bytes 8388608 | tf_op jit(solution)/shard_map/all_to_all | solution.py:32
  23.2 0.7 all-gather.6.cloned.1.call-update
  23.9 44.9 %all-to-all-done = bf16[8,64,4096]{2,1,0:T(8,128)(2,1)} async-done(((bf16[8,64,4096]{2,1,0:T(8,128)(2,1)}), bf16[8,64,4096]{2,1,0:T(8,128)(2,1)}, u32[]{:S(2)}, u32[]{:S(2)}) %all-to-all-start) | async-done | bytes 4194336 | tf_op jit(solution)/shard_map/all_to_all | solution.py:32
  68.9 7.8 %all_to_all.22 = bf16[512,4,1024]{2,1,0:T(4,128)(2,1)} reshape(bf16[8,64,4096]{2,1,0:T(8,128)(2,1)} %all-to-all-done) | data formatting | bytes 8388608 | tf_op jit(solution)/shard_map/all_to_all | solution.py:57
  76.7 5.5 %copy.10 = bf16[512,4,1024]{2,0,1:T(8,128)(2,1)} copy(bf16[512,4,1024]{2,1,0:T(4,128)(2,1)} %all_to_all.22) | data formatting | bytes 8388608 | tf_op jit(solution)/shard_map/all_to_all | solution.py:57
  82.2 5.8 %all-to-all-start.2 = ((bf16[512,4,1024]{2,0,1:T(8,128)(2,1)}), bf16[512,4,1024]{2,0,1:T(8,128)(2,1)}, u32[]{:S(2)}, u32[]{:S(2)}) async-start(bf16[512,4,1024]{2,0,1:T(8,128)(2,1)} %copy.10), calls=%async_computation.2 | async-start | bytes 8388608 | tf_op jit(solution)/shard_map/all_to_all | solution.py:57
  88.0 4.2 all-gather.4.cloned.1.call-done
  92.2 194.6 %all-to-all-done.2 = bf16[512,4,1024]{2,0,1:T(8,128)(2,1)} async-done(((bf16[512,4,1024]{2,0,1:T(8,128)(2,1)}), bf16[512,4,1024]{2,0,1:T(8,128)(2,1)}, u32[]{:S(2)}, u32[]{:S(2)}) %all-to-all-start.2) | async-done | bytes 4194336 | tf_op jit(solution)/shard_map/all_to_all | solution.py:57
  286.8 10.7 %fusion.19 = (bf16[1024,1024]{1,0:T(8,128)(2,1)}, f32[1024,1024]{1,0:T(8,128)}) fusion(bf16[2048,1024]{1,0:T(8,128)(2,1)} %bitcast.12, bf16[2048,1024]{1,0:T(8,128)(2,1)} %all-gather.4.cloned.1.call-done), kind=kOutput, calls=%fused_computation.29 | convolution fusion | flops 4296015872 | bytes 14680064 | tf_op jit(solution)/shard_map/dot_general | solution.py:59
  297.5 60.1 %collective-permute-done = bf16[1024,1024]{1,0:T(8,128)(2,1)S(1)} collective-permute-done((bf16[1024,1024]{1,0:T(8,128)(2,1)}, bf16[1024,1024]{1,0:T(8,128)(2,1)S(1)}, u32[]{:S(2)}, u32[]{:S(2)}) %collective-permute-start) | collective-permute-done | bytes 2097184 | tf_op jit(solution)/shard_map/ppermute | solution.py:12
  357.6 7.0 %convert_select_fusion.1 = (f32[1024,1024]{1,0:T(8,128)}, f32[1024,1024]{1,0:T(8,128)}) fusion(f32[1024,1024]{1,0:T(8,128)} %get-tuple-element.6, bf16[1024,1024]{1,0:T(8,128)(2,1)S(1)} %collective-permute-done, pred[]{:T(512)S(6)} %eq.38), kind=kLoop, calls=%fused_computation.11 | loop fusion | flops 3145728 | bytes 14680065 | tf_op jit(solution)/shard_map/jit(_where)/select_n | solution.py:68
  364.6 10.2 %fusion.8 = bf16[512,1024]{1,0:T(8,128)(2,1)} fusion(bf16[512,4096]{1,0:T(8,128)(2,1)} %bitcast.7, bf16[1,1024,4096]{2,1,0:T(8,128)(2,1)} %all-gather.6.cloned.1.call-done), kind=kOutput, calls=%fused_computation.16 | convolution fusion | flops 4295491584 | bytes 13631488 | tf_op jit(solution)/shard_map/dot_general | solution.py:41
  374.9 7.8 %all-to-all-start.1 = ((bf16[8,64,1024]{2,1,0:T(8,128)(2,1)}), bf16[8,64,1024]{2,1,0:T(8,128)(2,1)S(1)}, u32[]{:S(2)}, u32[]{:S(2)}) async-start(bf16[8,64,1024]{2,1,0:T(8,128)(2,1)} %bitcast.9), calls=%async_computation.1 | async-start | bytes 2097152 | tf_op jit(solution)/shard_map/all_to_all | solution.py:47
  382.7 33.1 %bitcast_add_fusion = f32[1,1024,2048]{2,1,0:T(8,128)} fusion(f32[1,1024,2048]{2,1,0:T(8,128)} %param.11, f32[1024,1024]{1,0:T(8,128)} %get-tuple-element.6, f32[1024,1024]{1,0:T(8,128)} %get-tuple-element.4, f32[1024,1024]{1,0:T(8,128)} %get-tuple-element.3), kind=kOutput, calls=%fused_computation.5 | convolution fusion | flops 25778192384 | bytes 29360128 | tf_op jit(solution)/shard_map/dot_general | solution.py:74
  415.8 15.1 %bitcast_add_fusion.1 = f32[1,512,1024]{2,1,0:T(8,128)} fusion(f32[1,512,1024]{2,1,0:T(8,128)S(1)} %copy-done.2, f32[1024,1024]{1,0:T(8,128)S(1)} %copy-done.1, f32[1024,1024]{1,0:T(8,128)S(1)} %copy-done, s32[]{:T(128)S(6)} %select_n.32), kind=kOutput, calls=%fused_computation.13 | convolution fusion | flops 12889620480 | bytes 20971524 | tf_op jit(solution)/shard_map/dot_general | solution.py:86
  430.9 2.0 gather_fusion
  (13 shorter events, 0.1 us)
Async XLA Ops:
  7.2 85.1 %all-gather.4.cloned.1.call-start = ((), (), s32[]{:S(2)}) async-start(), calls=%async_computation.3 | async-start | bytes 5242880 | tf_op jit(solution)/shard_map/all_gather | solution.py:61
  18.0 50.9 %all-to-all-start = ((bf16[8,64,4096]{2,1,0:T(8,128)(2,1)}), bf16[8,64,4096]{2,1,0:T(8,128)(2,1)}, u32[]{:S(2)}, u32[]{:S(2)}) async-start(bf16[8,64,4096]{2,1,0:T(8,128)(2,1)} %bitcast.34), calls=%async_computation | async-start | bytes 8388608 | tf_op jit(solution)/shard_map/all_to_all | solution.py:32
  23.2 341.4 %all-gather.6.cloned.1.call-start = ((), (), s32[]{:S(2)}) async-start(), calls=%async_computation.4 | async-start | bytes 10485760 | tf_op jit(solution)/shard_map/all_gather | solution.py:43
  82.2 204.6 %all-to-all-start.2 = ((bf16[512,4,1024]{2,0,1:T(8,128)(2,1)}), bf16[512,4,1024]{2,0,1:T(8,128)(2,1)}, u32[]{:S(2)}, u32[]{:S(2)}) async-start(bf16[512,4,1024]{2,0,1:T(8,128)(2,1)} %copy.10), calls=%async_computation.2 | async-start | bytes 8388608 | tf_op jit(solution)/shard_map/all_to_all | solution.py:57
  297.5 60.1 %collective-permute-start = (bf16[1024,1024]{1,0:T(8,128)(2,1)}, bf16[1024,1024]{1,0:T(8,128)(2,1)S(1)}, u32[]{:S(2)}, u32[]{:S(2)}) collective-permute-start(bf16[1024,1024]{1,0:T(8,128)(2,1)} %get-tuple-element.5), channel_id=1, source_target_pairs={{0,8},{8,0},{16,24},{24,16},{1,9},{9,1},{17,25},{25,17},{2,10},{10... | collective-permute-start | bytes 6291464 | tf_op jit(solution)/shard_map/ppermute | solution.py:12
  374.9 56.1 %all-to-all-start.1 = ((bf16[8,64,1024]{2,1,0:T(8,128)(2,1)}), bf16[8,64,1024]{2,1,0:T(8,128)(2,1)S(1)}, u32[]{:S(2)}, u32[]{:S(2)}) async-start(bf16[8,64,1024]{2,1,0:T(8,128)(2,1)} %bitcast.9), calls=%async_computation.1 | async-start | bytes 2097152 | tf_op jit(solution)/shard_map/all_to_all | solution.py:47
  382.7 33.1 %copy-start = (f32[1024,1024]{1,0:T(8,128)S(1)}, f32[1024,1024]{1,0:T(8,128)}, u32[]{:S(2)}) copy-start(f32[1024,1024]{1,0:T(8,128)} %get-tuple-element.3) | copy-start | bytes 12582916
  382.7 33.1 %copy-start.1 = (f32[1024,1024]{1,0:T(8,128)S(1)}, f32[1024,1024]{1,0:T(8,128)}, u32[]{:S(2)}) copy-start(f32[1024,1024]{1,0:T(8,128)} %get-tuple-element.4) | copy-start | bytes 12582916
  382.7 33.1 %copy-start.2 = (f32[1,512,1024]{2,1,0:T(8,128)S(1)}, f32[1,512,1024]{2,1,0:T(8,128)}, u32[]{:S(2)}) copy-start(f32[1,512,1024]{2,1,0:T(8,128)} %param.10) | copy-start | bytes 6291460
Sparse Core Ops, SparseCore 0:
  9.5 82.6 all-gather.3
  93.8 223.5 all-gather.5
where the time goes:
time: 446 us; the launch traced here: 440 us
  waiting for transfers between devices  305 us (68%)
  matrix products  69.1 us (15%)
  local copies, waits for them, and re-layouts  22.6 us (5%)
  starting transfers between devices  18.9 us (4%)
  between operations  14.3 us (3%)
  other arithmetic  9.75 us (2%)
    all_to_all x1, waiting for transfers between devices, local(): lax.all_to_all(arrived, 'dp', split_axis=1, concat_axis=0, tiled=True)  195 us
    ppermute x1, waiting for transfers between devices, swapped(): return lax.ppermute(value, axis, pairs)  60.1 us
    all_to_all x1, waiting for transfers between devices, local(): lax.all_to_all(outgoing.reshape(expert_count, capacity, model_width), 'ex...  44.9 us
    dot_general x1, matrix products, local(): lax.dot_general(own_piece, block_grad, (((1,), (1,)), ((), ())), precisio...  33.1 us
    dot_general x1, matrix products, local(): lax.dot_general(hidden_cols, block_grad, (((0,), (0,)), ((), ())), precis...  15.1 us
    all_to_all x2, local copies, waits for them, and re-layouts, local(): lax.all_to_all(arrived, 'dp', split_axis=1, concat_axis=0, tiled=True)  13.3 us
    dot_general x1, matrix products, local(): lax.dot_general(columns, lax.all_gather(hidden, 'dp', axis=0, tiled=True)...  10.7 us
    dot_general x1, matrix products, local(): lax.dot_general(columns, lax.all_gather(weight[0], 'dp', axis=1, tiled=Tr...  10.2 us
  transfers between devices with their start and end apart: 6, of which 4 were waited for; matrix products, arithmetic and copies ran while one was open for 19% of the time, Pallas kernels for 0%

commit v1 on v0

--- a/solution.py
+++ b/solution.py
@@ -2,8 +2,35 @@
 import jax.numpy as jnp
 from jax import lax
 from jax.sharding import PartitionSpec as P
+from jax.lax import axis_index, axis_size, ppermute
 
 ema_decay = 0.9
+
+
+def obtain_the_halves(target, row_dim, point):
+    reply = target.shape
+    tmp = target.reshape(*reply[:row_dim], point, reply[row_dim] // point, *reply[row_dim + 1 :])
+    return jnp.moveaxis(tmp, row_dim, 0)
+
+
+def convert_vector(array_in, ndim_at):
+    e_now = list(array_in.shape[1:])
+    e_now[ndim_at] *= array_in.shape[0]
+    return jnp.moveaxis(array_in, 0, ndim_at).reshape(e_now)
+
+
+def _tell_shards(load, bus_axis, local_values, values):
+    current_value = axis_size(bus_axis)
+    h_now = axis_index(bus_axis)
+    known, view_out = (current_value, h_now)
+    mat_out = obtain_the_halves(load, local_values, known)
+    table = [mat_out[view_out]]
+    for hop_no in range(1, known):
+        now = mat_out[view_out ^ hop_no]
+        table.append(ppermute(now, bus_axis, [(h, h ^ hop_no) for h in range(known)]))
+    carry = jnp.stack(table)
+    mat_out = carry[view_out ^ jnp.arange(known)]
+    return convert_vector(mat_out, values)
 
 
 def swapped(value, axis, distance):
@@ -29,13 +56,7 @@
     capacity = slot_count // expert_count
     target_slots = slot_places(destination[:, 0], expert_count, capacity)
     outgoing = jnp.zeros((slot_count, model_width), out_grad.dtype).at[target_slots].set(out_grad)
-    arrived = lax.all_to_all(
-        outgoing.reshape(expert_count, capacity, model_width),
-        "expert",
-        split_axis=0,
-        concat_axis=0,
-        tiled=True,
-    )
+    arrived = _tell_shards(outgoing.reshape(expert_count, capacity, model_width), "expert", 0, 0)
     arrived = arrived.reshape(slot_count, model_width)
     columns = arrived
     slot_grad = lax.dot_general(

time: 446 us -> 459 us (1.029)
  local copies, waits for them, and re-layouts: 22.6 us -> 38 us
  waiting for transfers between devices: 305 us -> 299 us
    all_to_all x1 -> x0, waiting for transfers between devices: 44.9 us -> none  [local(): lax.all_to_all(outgoing.reshape(expert_count, capacity, model_width), 'ex...]
    ppermute x0 -> x7, waiting for transfers between devices: none -> 37 us  [_tell_shards(): ppermute(now, bus_axis, [(h, h ^ hop_no) for h in range(known)])]
    ppermute x0 -> x7, starting transfers between devices: none -> 10.4 us  [_tell_shards(): ppermute(now, bus_axis, [(h, h ^ hop_no) for h in range(known)])]
    all_to_all x1 -> x0, starting transfers between devices: 5.21 us -> none  [local(): lax.all_to_all(outgoing.reshape(expert_count, capacity, model_width), 'ex...]
    all_to_all x1, waiting for transfers between devices: 195 us -> 200 us  [local(): lax.all_to_all(arrived, 'dp', split_axis=1, concat_axis=0, tiled=True)]
    unnamed x6 -> x12, local copies, waits for them, and re-layouts: 0.01 us -> 5.09 us
    gather x0 -> x1, local copies, waits for them, and re-layouts: none -> 5.01 us  [_tell_shards(): mat_out = carry[view_out ^ jnp.arange(known)]]
  transfers between devices with their start and end apart: 6 -> 12, of which waited for: 4 -> 5; matrix products, arithmetic and copies ran while one was open for 19% -> 21% of each run, Pallas kernels for 0% -> 0%
where the time goes in v1:
time: 459 us; the launch traced here: 452 us
  waiting for transfers between devices  299 us (65%)
  matrix products  69 us (15%)
  local copies, waits for them, and re-layouts  38 us (8%)
  starting transfers between devices  21.9 us (5%)
  between operations  14.4 us (3%)
  other arithmetic  9.75 us (2%)
    all_to_all x1, waiting for transfers between devices, local(): lax.all_to_all(arrived, 'dp', split_axis=1, concat_axis=0, tiled=True)  200 us
    ppermute x1, waiting for transfers between devices, swapped(): return lax.ppermute(value, axis, pairs)  61.4 us
    ppermute x7, waiting for transfers between devices, _tell_shards(): ppermute(now, bus_axis, [(h, h ^ hop_no) for h in range(known)])  37 us
    dot_general x1, matrix products, local(): lax.dot_general(own_piece, block_grad, (((1,), (1,)), ((), ())), precisio...  33.1 us
    dot_general x1, matrix products, local(): lax.dot_general(hidden_cols, block_grad, (((0,), (0,)), ((), ())), precis...  15.1 us
    all_to_all x2, local copies, waits for them, and re-layouts, local(): lax.all_to_all(arrived, 'dp', split_axis=1, concat_axis=0, tiled=True)  13.3 us
    dot_general x1, matrix products, local(): lax.dot_general(columns, lax.all_gather(hidden, 'dp', axis=0, tiled=True)...  10.7 us
    ppermute x7, starting transfers between devices, _tell_shards(): ppermute(now, bus_axis, [(h, h ^ hop_no) for h in range(known)])  10.4 us
  transfers between devices with their start and end apart: 12, of which 5 were waited for; matrix products, arithmetic and copies ran while one was open for 21% of the time, Pallas kernels for 0%

profile of v1, /device:TPU:1, one launch (start us, length us, event | category | flops | bytes accessed | tf_op | source)
XLA Modules:
  0.0 452.0 jit_solution(1144426905658835822)
XLA Ops:
  11.0 7.1 %scatter_custom_fusion = bf16[512,4096]{1,0:T(8,128)(2,1)} fusion(s32[256]{0:T(256)S(1)} %bitcast.69, bf16[256,4096]{1,0:T(8,128)(2,1)} %param.6, bf16[]{:T(256)} %constant.18.clone.1), kind=kCustom, calls=%fused_computation.15 | custom fusion | bytes 4194816 | tf_op jit(solution)/shard_map/scatter | solution.py:58
  18.1 4.5 dynamic-slice_bitcast_fusion
  22.6 2.6 collective-permute-start.1
  25.2 1.7 collective-permute-start.3
  27.3 2.5 collective-permute-start.5
  29.8 0.9 bitcast_dynamic-update-slice_fusion.6
  30.6 7.1 %collective-permute-done.1 = bf16[1,64,4096]{2,1,0:T(8,128)(2,1)S(1)} collective-permute-done((bf16[1,64,4096]{2,1,0:T(8,128)(2,1)}, bf16[1,64,4096]{2,1,0:T(8,128)(2,1)S(1)}, u32[]{:S(2)}, u32[]{:S(2)}) %collective-permute-start.1) | collective-permute-done | bytes 524320 | tf_op jit(solution)/shard_map/ppermute | solution.py:30
  37.8 3.3 collective-permute-start.6
  41.9 7.5 %collective-permute-done.2 = bf16[1,64,4096]{2,1,0:T(8,128)(2,1)S(1)} collective-permute-done((bf16[1,64,4096]{2,1,0:T(8,128)(2,1)}, bf16[1,64,4096]{2,1,0:T(8,128)(2,1)S(1)}, u32[]{:S(2)}, u32[]{:S(2)}) %collective-permute-start.2) | collective-permute-done | bytes 524320 | tf_op jit(solution)/shard_map/ppermute | solution.py:30
  51.1 22.3 %collective-permute-done.4 = bf16[1,64,4096]{2,1,0:T(8,128)(2,1)S(1)} collective-permute-done((bf16[1,64,4096]{2,1,0:T(8,128)(2,1)}, bf16[1,64,4096]{2,1,0:T(8,128)(2,1)S(1)}, u32[]{:S(2)}, u32[]{:S(2)}) %collective-permute-start.4) | collective-permute-done | bytes 524320 | tf_op jit(solution)/shard_map/ppermute | solution.py:30
  75.9 5.0 %gather_fusion = bf16[8,64,4096]{2,1,0:T(8,128)(2,1)} fusion(bf16[8,64,4096]{2,1,0:T(8,128)(2,1)} %bitcast.66, s32[1024]{0:T(1024)S(1)} %pad_clamp_fusion.1), kind=kCustom, calls=%fused_computation | custom fusion | bytes 8388640 | tf_op jit(solution)/shard_map/gather | solution.py:32
  80.9 7.8 %all_to_all.18 = bf16[512,4,1024]{2,1,0:T(4,128)(2,1)} reshape(bf16[8,64,4096]{2,1,0:T(8,128)(2,1)} %gather_fusion) | data formatting | bytes 8388608 | tf_op jit(solution)/shard_map/all_to_all | solution.py:78
  88.8 5.5 %copy.10 = bf16[512,4,1024]{2,0,1:T(8,128)(2,1)} copy(bf16[512,4,1024]{2,1,0:T(4,128)(2,1)} %all_to_all.18) | data formatting | bytes 8388608 | tf_op jit(solution)/shard_map/all_to_all | solution.py:78
  94.2 5.3 %all-to-all-start.1 = ((bf16[512,4,1024]{2,0,1:T(8,128)(2,1)}), bf16[512,4,1024]{2,0,1:T(8,128)(2,1)}, u32[]{:S(2)}, u32[]{:S(2)}) async-start(bf16[512,4,1024]{2,0,1:T(8,128)(2,1)} %copy.10), calls=%async_computation.1 | async-start | bytes 8388608 | tf_op jit(solution)/shard_map/all_to_all | solution.py:78
  99.6 199.7 %all-to-all-done.1 = bf16[512,4,1024]{2,0,1:T(8,128)(2,1)} async-done(((bf16[512,4,1024]{2,0,1:T(8,128)(2,1)}), bf16[512,4,1024]{2,0,1:T(8,128)(2,1)}, u32[]{:S(2)}, u32[]{:S(2)}) %all-to-all-start.1) | async-done | bytes 4194336 | tf_op jit(solution)/shard_map/all_to_all | solution.py:78
  299.3 10.7 %fusion.20 = (bf16[1024,1024]{1,0:T(8,128)(2,1)}, f32[1024,1024]{1,0:T(8,128)}) fusion(bf16[2048,1024]{1,0:T(8,128)(2,1)} %bitcast.28, bf16[2048,1024]{1,0:T(8,128)(2,1)} %all-gather.4.cloned.1.call-done), kind=kOutput, calls=%fused_computation.48 | convolution fusion | flops 4296015872 | bytes 14680064 | tf_op jit(solution)/shard_map/dot_general | solution.py:80
  310.0 1.6 collective-permute-start.7
  311.6 61.4 %collective-permute-done.7 = bf16[1024,1024]{1,0:T(8,128)(2,1)S(1)} collective-permute-done((bf16[1024,1024]{1,0:T(8,128)(2,1)}, bf16[1024,1024]{1,0:T(8,128)(2,1)S(1)}, u32[]{:S(2)}, u32[]{:S(2)}) %collective-permute-start.7) | collective-permute-done | bytes 2097184 | tf_op jit(solution)/shard_map/ppermute | solution.py:39
  373.1 7.0 %convert_select_fusion.1 = (f32[1024,1024]{1,0:T(8,128)}, f32[1024,1024]{1,0:T(8,128)}) fusion(f32[1024,1024]{1,0:T(8,128)} %get-tuple-element.14, bf16[1024,1024]{1,0:T(8,128)(2,1)S(1)} %collective-permute-done.7, pred[]{:T(512)S(6)} %eq.38), kind=kLoop, calls=%fused_computation.12 | loop fusion | flops 3145728 | bytes 14680065 | tf_op jit(solution)/shard_map/jit(_where)/select_n | solution.py:89
  380.1 10.1 %fusion.8 = bf16[512,1024]{1,0:T(8,128)(2,1)} fusion(bf16[512,4096]{1,0:T(8,128)(2,1)} %bitcast.64, bf16[1,1024,4096]{2,1,0:T(8,128)(2,1)} %all-gather.6.cloned.1.call-done), kind=kOutput, calls=%fused_computation.17 | convolution fusion | flops 4295491584 | bytes 13631488 | tf_op jit(solution)/shard_map/dot_general | solution.py:62
  390.2 4.5 all-to-all-start
  394.8 33.1 %bitcast_add_fusion = f32[1,1024,2048]{2,1,0:T(8,128)} fusion(f32[1,1024,2048]{2,1,0:T(8,128)} %param.11, f32[1024,1024]{1,0:T(8,128)} %get-tuple-element.14, f32[1024,1024]{1,0:T(8,128)} %get-tuple-element.4, f32[1024,1024]{1,0:T(8,128)} %get-tuple-element.3), kind=kOutput, calls=%fused_computation.6 | convolution fusion | flops 25778192384 | bytes 29360128 | tf_op jit(solution)/shard_map/dot_general | solution.py:95
  427.9 15.1 %bitcast_add_fusion.1 = f32[1,512,1024]{2,1,0:T(8,128)} fusion(f32[1,512,1024]{2,1,0:T(8,128)S(1)} %copy-done.2, f32[1024,1024]{1,0:T(8,128)S(1)} %copy-done.1, f32[1024,1024]{1,0:T(8,128)S(1)} %copy-done, s32[]{:T(128)S(6)} %select_n.75), kind=kOutput, calls=%fused_computation.14 | convolution fusion | flops 12889620480 | bytes 20971524 | tf_op jit(solution)/shard_map/dot_general | solution.py:107
  443.0 2.0 gather_fusion.1
  (36 shorter events, 9.2 us)
Async XLA Ops:
  7.2 92.4 %all-gather.4.cloned.1.call-start = ((), (), s32[]{:S(2)}) async-start(), calls=%async_computation.2 | async-start | bytes 5242880 | tf_op jit(solution)/shard_map/all_gather | solution.py:82
  7.9 372.2 %all-gather.6.cloned.1.call-start = ((), (), s32[]{:S(2)}) async-start(), calls=%async_computation.3 | async-start | bytes 10485760 | tf_op jit(solution)/shard_map/all_gather | solution.py:64
  22.6 4.7 %collective-permute-start = (bf16[1,64,4096]{2,1,0:T(8,128)(2,1)}, bf16[1,64,4096]{2,1,0:T(8,128)(2,1)S(1)}, u32[]{:S(2)}, u32[]{:S(2)}) collective-permute-start(bf16[1,64,4096]{2,1,0:T(8,128)(2,1)} %get-tuple-element.11), channel_id=1, source_target_pairs={{0,1},{1,0},{2,3},{3,2},{4,5},{5,4},{6,7},{7,6},{8,9},{9,8},{10,11... | collective-permute-start | bytes 1572872 | tf_op jit(solution)/shard_map/ppermute | solution.py:30
  22.6 15.2 %collective-permute-start.1 = (bf16[1,64,4096]{2,1,0:T(8,128)(2,1)}, bf16[1,64,4096]{2,1,0:T(8,128)(2,1)S(1)}, u32[]{:S(2)}, u32[]{:S(2)}) collective-permute-start(bf16[1,64,4096]{2,1,0:T(8,128)(2,1)} %get-tuple-element.10), channel_id=1, source_target_pairs={{0,2},{1,3},{2,0},{3,1},{4,6},{5,7},{6,4},{7,5},{8,10},{9,11},{10,... | collective-permute-start | bytes 1572872 | tf_op jit(solution)/shard_map/ppermute | solution.py:30
  25.2 24.2 %collective-permute-start.2 = (bf16[1,64,4096]{2,1,0:T(8,128)(2,1)}, bf16[1,64,4096]{2,1,0:T(8,128)(2,1)S(1)}, u32[]{:S(2)}, u32[]{:S(2)}) collective-permute-start(bf16[1,64,4096]{2,1,0:T(8,128)(2,1)} %get-tuple-element.9), channel_id=1, source_target_pairs={{0,3},{1,2},{2,1},{3,0},{4,7},{5,6},{6,5},{7,4},{8,11},{9,10},{10,... | collective-permute-start | bytes 1572872 | tf_op jit(solution)/shard_map/ppermute | solution.py:30
  25.2 25.1 %collective-permute-start.3 = (bf16[1,64,4096]{2,1,0:T(8,128)(2,1)}, bf16[1,64,4096]{2,1,0:T(8,128)(2,1)S(1)}, u32[]{:S(2)}, u32[]{:S(2)}) collective-permute-start(bf16[1,64,4096]{2,1,0:T(8,128)(2,1)} %get-tuple-element.8), channel_id=1, source_target_pairs={{0,4},{1,5},{2,6},{3,7},{4,0},{5,1},{6,2},{7,3},{8,12},{9,13},{10,... | collective-permute-start | bytes 1572872 | tf_op jit(solution)/shard_map/ppermute | solution.py:30
  26.9 46.5 %collective-permute-start.4 = (bf16[1,64,4096]{2,1,0:T(8,128)(2,1)}, bf16[1,64,4096]{2,1,0:T(8,128)(2,1)S(1)}, u32[]{:S(2)}, u32[]{:S(2)}) collective-permute-start(bf16[1,64,4096]{2,1,0:T(8,128)(2,1)} %get-tuple-element.7), channel_id=1, source_target_pairs={{0,5},{1,4},{2,7},{3,6},{4,1},{5,0},{6,3},{7,2},{8,13},{9,12},{10,... | collective-permute-start | bytes 1572872 | tf_op jit(solution)/shard_map/ppermute | solution.py:30
  27.3 46.9 %collective-permute-start.5 = (bf16[1,64,4096]{2,1,0:T(8,128)(2,1)}, bf16[1,64,4096]{2,1,0:T(8,128)(2,1)S(1)}, u32[]{:S(2)}, u32[]{:S(2)}) collective-permute-start(bf16[1,64,4096]{2,1,0:T(8,128)(2,1)} %get-tuple-element.6), channel_id=1, source_target_pairs={{0,6},{1,7},{2,4},{3,5},{4,2},{5,3},{6,0},{7,1},{8,14},{9,15},{10,... | collective-permute-start | bytes 1572872 | tf_op jit(solution)/shard_map/ppermute | solution.py:30
  37.8 37.3 %collective-permute-start.6 = (bf16[1,64,4096]{2,1,0:T(8,128)(2,1)S(1)}, bf16[1,64,4096]{2,1,0:T(8,128)(2,1)S(1)}, u32[]{:S(2)}, u32[]{:S(2)}) collective-permute-start(bf16[1,64,4096]{2,1,0:T(8,128)(2,1)S(1)} %get-tuple-element.5), channel_id=1, source_target_pairs={{0,7},{1,6},{2,5},{3,4},{4,3},{5,2},{6,1},{7,0},{8,15},{9,14},{10,... | collective-permute-start | bytes 1572872 | tf_op jit(solution)/shard_map/ppermute | solution.py:30
  94.2 205.1 %all-to-all-start.1 = ((bf16[512,4,1024]{2,0,1:T(8,128)(2,1)}), bf16[512,4,1024]{2,0,1:T(8,128)(2,1)}, u32[]{:S(2)}, u32[]{:S(2)}) async-start(bf16[512,4,1024]{2,0,1:T(8,128)(2,1)} %copy.10), calls=%async_computation.1 | async-start | bytes 8388608 | tf_op jit(solution)/shard_map/all_to_all | solution.py:78
  310.0 63.1 %collective-permute-start.7 = (bf16[1024,1024]{1,0:T(8,128)(2,1)}, bf16[1024,1024]{1,0:T(8,128)(2,1)S(1)}, u32[]{:S(2)}, u32[]{:S(2)}) collective-permute-start(bf16[1024,1024]{1,0:T(8,128)(2,1)} %get-tuple-element.13), channel_id=1, source_target_pairs={{0,8},{8,0},{16,24},{24,16},{1,9},{9,1},{17,25},{25,17},{2,10},{10... | collective-permute-start | bytes 6291464 | tf_op jit(solution)/shard_map/ppermute | solution.py:39
  390.2 52.8 %all-to-all-start = ((bf16[8,64,1024]{2,1,0:T(8,128)(2,1)}), bf16[8,64,1024]{2,1,0:T(8,128)(2,1)S(1)}, u32[]{:S(2)}, u32[]{:S(2)}) async-start(bf16[8,64,1024]{2,1,0:T(8,128)(2,1)} %bitcast.25), calls=%async_computation | async-start | bytes 2097152 | tf_op jit(solution)/shard_map/all_to_all | solution.py:68
  394.7 33.1 %copy-start = (f32[1024,1024]{1,0:T(8,128)S(1)}, f32[1024,1024]{1,0:T(8,128)}, u32[]{:S(2)}) copy-start(f32[1024,1024]{1,0:T(8,128)} %get-tuple-element.3) | copy-start | bytes 12582916
  394.8 33.1 %copy-start.1 = (f32[1024,1024]{1,0:T(8,128)S(1)}, f32[1024,1024]{1,0:T(8,128)}, u32[]{:S(2)}) copy-start(f32[1024,1024]{1,0:T(8,128)} %get-tuple-element.4) | copy-start | bytes 12582916
  394.8 33.1 %copy-start.2 = (f32[1,512,1024]{2,1,0:T(8,128)S(1)}, f32[1,512,1024]{2,1,0:T(8,128)}, u32[]{:S(2)}) copy-start(f32[1,512,1024]{2,1,0:T(8,128)} %param.10) | copy-start | bytes 6291460
Sparse Core Ops, SparseCore 0:
  9.5 82.6 all-gather.3
  93.8 234.6 all-gather.5
